TPU v7x, 32 devices: a whole 2x2x4 slice. The times are simulated.
32 devices in a mesh: row: 4 (over y, x), col: 8 (over z, core).
Axes of the slice: x: 2, y: 2, z: 4, core: 2. Of those that a mesh axis runs over, the one named last changes fastest.
Arguments:
- inverse: float32 [24576, 24576], P('row', 'col'), may hold values from -0.0546875 to 0.0546875
- parent_panel: float32 [24576, 256], P(('row', 'col')), may hold values from -1.8 to 1.8
- child_panel: float32 [24576, 256], P(('row', 'col')), may hold values from -1.8 to 1.8
- child_top: float32 [256, 256], replicated, may hold values from -0.375 to 0.375
- diag_parent: float32 [256, 256], replicated, may hold values from -12 to 12
- diag_child: float32 [256, 256], replicated, may hold values from -12 to 12
- parent_blocks: int32 [192], replicated, may hold values from 0 to 1
- child_blocks: int32 [192], replicated, may hold values from 0 to 1, as said below
Outputs:
- parent_column: float32 [24576, 256], P(('row', 'col'))
- parent_diagonal: float32 [256, 256], replicated
- child_column: float32 [24576, 256], P(('row', 'col'))
- child_upper: float32 [256, 256], replicated
- child_diagonal: float32 [256, 256], replicated
Inputs may be any that keep to these rules, and one draw needn't show every extreme that they name: `child_blocks`: each entry is 0 or 1, and is 1 only where parent_blocks is 1.
All inputs are finite; a program needn't handle non-finite values.
Results may differ from a plain program's by a relative error of at most 0.000086.
Values sent between devices are 32-bit elements; how exact they have to be, the bound alone decides.
A program may use at most 192 MiB of HBM per device.

v0:
```python
import jax
import jax.numpy as jnp
from jax import lax
from jax.sharding import PartitionSpec as P

BLK = 128
HIGHEST = lax.Precision.HIGHEST


def spread(value, axis, source):
    kept = jnp.where(lax.axis_index(axis) == source, value, 0).astype(value.dtype)
    return lax.psum(kept, axis)


def matmul(left, right):
    return jnp.dot(left, right, precision=HIGHEST, preferred_element_type=jnp.float32)


def local_mask(blocks, rows_here):
    flags = jnp.repeat(blocks, BLK, total_repeat_length=blocks.shape[0] * BLK)
    device = lax.axis_index("row") * lax.axis_size("col") + lax.axis_index("col")
    local_flags = lax.dynamic_slice_in_dim(flags, device * rows_here, rows_here, 0)
    return local_flags.astype(jnp.float32)[:, None]


def column_slice(block_rows, tile_cols):
    col_ratio = lax.axis_size("col") // lax.axis_size("row")
    index_col = lax.axis_index("col")
    wanted = lax.dynamic_slice_in_dim(block_rows, index_col % col_ratio * tile_cols, tile_cols, 0)
    return (wanted, index_col // col_ratio)


def apply_inverse(inverse, panel):
    rows_here = panel.shape[0]
    block_rows = lax.all_gather(panel, "col", axis=0, tiled=True)
    wanted, owner_row = column_slice(block_rows, inverse.shape[1])
    column_rows = spread(wanted, "row", owner_row)
    return lax.psum_scatter(
        matmul(lax.slice_in_dim(inverse, 0, rows_here * lax.axis_size("col"), axis=0), column_rows),
        "col",
        scatter_dimension=0,
        tiled=True,
    )


def per_device(
    inverse,
    parent_panel,
    child_panel,
    child_top,
    diag_parent,
    diag_child,
    parent_blocks,
    child_blocks,
):
    rows_here = parent_panel.shape[0]
    parent_mask = local_mask(parent_blocks, rows_here)
    child_mask = local_mask(child_blocks, rows_here)
    parent_masked = parent_panel * parent_mask
    child_masked = child_panel * child_mask
    parent_image = apply_inverse(inverse, parent_masked)
    child_image = apply_inverse(inverse, child_masked)
    parent_column = -(parent_mask * parent_image)
    parent_local = matmul(parent_masked.T, parent_column)
    cross_local = matmul(parent_column.T, child_masked)
    carried = matmul(parent_column, child_top)
    child_column = -(child_mask * (carried + child_image))
    image_local = matmul(child_masked.T, child_image)
    parent_sum, cross_sum, image_sum = lax.psum(
        (parent_local, cross_local, image_local), ("row", "col")
    )
    parent_diagonal = diag_parent - parent_sum
    child_upper = -(matmul(parent_diagonal, child_top) + cross_sum)
    child_diagonal = (
        diag_child - matmul(child_top.T, child_upper) + matmul(cross_sum.T, child_top) + image_sum
    )
    return (parent_column, parent_diagonal, child_column, child_upper, child_diagonal)


def solution(mesh):
    placed = (
        P("row", "col"),
        P(("row", "col"), None),
        P(("row", "col"), None),
        P(),
        P(),
        P(),
        P(),
        P(),
    )
    return jax.shard_map(
        per_device,
        mesh=mesh,
        in_specs=placed,
        out_specs=(P(("row", "col"), None), P(), P(("row", "col"), None), P(), P()),
        check_vma=False,
    )
```

profile of v0, /device:TPU:0, one launch (start us, length us, event | category | flops | bytes accessed | tf_op | source)
XLA Modules:
  0.0 949.8 jit_solution(11591505820948566814)
XLA Ops:
  7.3 0.8 add_bitcast_fusion.1
  8.0 1.9 scatter_custom_fusion
  10.2 0.3 reduce-window.21
  11.1 151.8 %gather_fusion = s32[24576]{0:T(1024)S(1)} fusion(s32[192]{0:T(256)S(1)} %copy-done.1, s32[24576]{0:T(1024)S(1)} %fusion.5), kind=kCustom, calls=%fused_computation.clone | custom fusion | bytes 294912 | tf_op jit(solution)/shard_map/jit(_take)/gather | solution.py:20
  162.9 151.8 %gather_fusion.1 = s32[24576]{0:T(1024)S(1)} fusion(s32[192]{0:T(256)S(1)} %copy-done.2, s32[24576]{0:T(1024)S(1)} %fusion.5), kind=kCustom, calls=%fused_computation.1.clone | custom fusion | bytes 294912 | tf_op jit(solution)/shard_map/jit(_take)/gather | solution.py:20
  314.8 0.3 copy.25
  315.1 0.9 broadcast_multiply_fusion
  316.2 0.3 copy.24
  316.4 0.9 broadcast_multiply_fusion.1
  317.5 66.2 %all-gather.5.cloned.1.call-done = f32[6144,256]{0,1:T(8,128)} async-done(((f32[768,256]{0,1:T(8,128)}), f32[6144,256]{0,1:T(8,128)}) %all-gather.5.cloned.1.call-update) | async-done | bytes 6291472 | tf_op jit(solution)/shard_map/all_gather | solution.py:35
  383.7 3.8 dynamic-slice_select_fusion
  387.5 61.7 %all-gather.3.cloned.1.call-done = f32[6144,256]{0,1:T(8,128)} async-done(((f32[768,256]{0,1:T(8,128)}), f32[6144,256]{0,1:T(8,128)}) %all-gather.3.cloned.1.call-update) | async-done | bytes 6291472 | tf_op jit(solution)/shard_map/all_gather | solution.py:35
  449.2 3.9 dynamic-slice_select_fusion.1
  453.2 136.9 %all-reduce.9.cloned.1.call-done = (f32[3072,256]{0,1:T(8,128)}, f32[3072,256]{0,1:T(8,128)}) async-done(((f32[3072,256]{0,1:T(8,128)}, f32[3072,256]{0,1:T(8,128)}), (f32[3072,256]{0,1:T(8,128)}, f32[3072,256]{0,1:T(8,128)})) %all-reduce.9.cloned.1.call-update) | async-done | bytes 6291472 | tf_op jit(solution)/shard_map/psum | solution.py:12
  590.1 70.0 %convolution_bitcast_fusion.1 = f32[6144,256]{0,1:T(8,128)} fusion(f32[3072,256]{0,1:T(8,128)} %get-tuple-element.39, f32[6144,3072]{1,0:T(8,128)} %param.14), kind=kOutput, calls=%fused_computation.4 | convolution fusion | flops 57982058496 | bytes 84934656 | tf_op jit(solution)/shard_map/dot_general | solution.py:16
  660.4 1.6 copy-done.5
  662.0 70.3 %convolution_bitcast_fusion = f32[6144,256]{0,1:T(8,128)} fusion(f32[3072,256]{0,1:T(8,128)S(1)} %copy-done.5, f32[6144,3072]{1,0:T(8,128)} %param.14), kind=kOutput, calls=%fused_computation.3 | convolution fusion | flops 57982058496 | bytes 84934656 | tf_op jit(solution)/shard_map/dot_general | solution.py:16
  732.3 0.3 all-reduce.7.cloned.1.call-start
  732.6 1.3 multiply_negate_fusion
  733.9 1.5 fusion.11
  735.5 1.5 fusion.10
  737.0 64.8 %reduce-scatter.5.cloned.1.call-done = f32[768,256]{0,1:T(8,128)} async-done(((f32[6144,256]{0,1:T(8,128)}), f32[768,256]{0,1:T(8,128)}) %reduce-scatter.5.cloned.1.call-update) | async-done | bytes 786448 | tf_op jit(solution)/shard_map/reduce_scatter | solution.py:38
  801.8 2.7 fusion.12
  804.8 1.1 copy.30
  805.9 0.9 fusion.1
  806.8 1.1 copy.31
  808.0 129.5 %all-reduce.7.cloned.1.call-done = (f32[256,256]{1,0:T(8,128)}, f32[256,256]{1,0:T(8,128)}, f32[256,256]{0,1:T(8,128)}) async-done(((f32[256,256]{1,0:T(8,128)}, f32[256,256]{1,0:T(8,128)}, f32[256,256]{0,1:T(8,128)}), (f32[256,256]{1,0:T(8,128)}, f32[256,256]{1,0:T(8,128)}, f32[256,256]{0,1:T(8,128)})) %all-reduce.7.cloned.1.call-update) | async-done | bytes 786448 | tf_op jit(solution)/shard_map/psum | solution.py:69
  937.5 1.0 sub.20
  938.4 1.4 fusion.4
  939.9 0.6 fusion.3
  940.5 1.6 fusion.2
  942.1 0.8 copy.32
  (55 shorter events, 1.6 us)
Async XLA Ops:
  7.2 798.7 %copy-start = (f32[256,256]{1,0:T(8,128)S(1)}, f32[256,256]{1,0:T(8,128)}, u32[]{:S(2)}) copy-start(f32[256,256]{1,0:T(8,128)} %param.17) | copy-start | bytes 786436
  7.2 3.9 copy-start.1
  7.2 376.5 %all-gather.5.cloned.1.call-start = ((), (), s32[]{:S(2)}) async-start(), calls=%async_computation.4 | async-start | bytes 7077888 | tf_op jit(solution)/shard_map/all_gather | solution.py:35
  11.1 151.8 %copy-start.2 = (s32[192]{0:T(256)S(1)}, s32[192]{0:T(256)}, u32[]{:S(2)}) copy-start(s32[192]{0:T(256)} %param.21) | copy-start | bytes 2308
  162.9 151.8 %copy-start.9 = (f32[768,256]{1,0:T(8,128)S(1)}, f32[768,256]{1,0:T(8,128)}, u32[]{:S(2)}) copy-start(f32[768,256]{1,0:T(8,128)} %param.16) | copy-start | bytes 2359300
  314.8 1.4 copy-start.10
  316.1 133.1 %all-gather.3.cloned.1.call-start = ((), (), s32[]{:S(2)}) async-start(), calls=%async_computation.2 | async-start | bytes 7077888 | tf_op jit(solution)/shard_map/all_gather | solution.py:35
  317.4 272.7 %all-reduce.9.cloned.1.call-start = ((), (), s32[]{:S(2)}) async-start(), calls=%async_computation.7 | async-start | bytes 12582912 | tf_op jit(solution)/shard_map/psum | solution.py:12
  453.1 279.4 %reduce-scatter.3.cloned.1.call-start = ((), (), s32[]{:S(2)}) async-start(), calls=%async_computation.3 | async-start | bytes 7077888 | tf_op jit(solution)/shard_map/reduce_scatter | solution.py:38
  660.1 1.9 copy-start.5
  660.1 141.7 %reduce-scatter.5.cloned.1.call-start = ((), (), s32[]{:S(2)}) async-start(), calls=%async_computation.5 | async-start | bytes 7077888 | tf_op jit(solution)/shard_map/reduce_scatter | solution.py:38
  732.3 1.7 copy-start.3
  732.3 3.2 copy-start.4
  732.3 205.2 %all-reduce.7.cloned.1.call-start = ((), (), s32[]{:S(2)}) async-start(), calls=%async_computation.6 | async-start | bytes 1572864 | tf_op jit(solution)/shard_map/psum | solution.py:69
  733.9 70.7 %copy-start.12 = (f32[256,256]{1,0:T(8,128)S(1)}, f32[256,256]{1,0:T(8,128)}, u32[]{:S(2)}) copy-start(f32[256,256]{1,0:T(8,128)} %param.19) | copy-start | bytes 786436
  801.8 4.1 copy-start.6
  804.6 132.8 %copy-start.11 = (f32[256,256]{1,0:T(8,128)S(1)}, f32[256,256]{1,0:T(8,128)}, u32[]{:S(2)}) copy-start(f32[256,256]{1,0:T(8,128)} %param.18) | copy-start | bytes 786436
  938.4 4.5 copy-start.7
  939.9 3.1 copy-start.8
Sparse Core Ops, SparseCore 0:
  316.2 67.4 all-gather.4
  385.9 63.3 all-gather.2
  453.3 136.7 all-reduce.8
  660.2 69.7 reduce-scatter.2
  732.4 69.4 reduce-scatter.4
  807.8 129.6 all-reduce.6
where the time goes:
time: 950 us
  waiting for transfers between devices  459 us (48%)
  local copies, waits for them, and re-layouts  310 us (33%)
  matrix products  151 us (16%)
  other arithmetic  15.3 us (2%)
  between operations  14.4 us (2%)
    gather x2, local copies, waits for them, and re-layouts, local_mask(): flags = jnp.repeat(blocks, BLK, total_repeat_length=blocks.shape[0] * BLK)  304 us
    dot_general x9, matrix products, matmul(): jnp.dot(left, right, precision=HIGHEST, preferred_element_type=jnp.float32)  151 us
    psum x1, waiting for transfers between devices, spread(): return lax.psum(kept, axis)  137 us
    psum x1, waiting for transfers between devices, per_device(): lax.psum((parent_local, cross_local, image_local), ('row', 'col'))  129 us
    all_gather x2, waiting for transfers between devices, apply_inverse(): block_rows = lax.all_gather(panel, 'col', axis=0, tiled=True)  128 us
    reduce_scatter x2, waiting for transfers between devices, apply_inverse(): lax.psum_scatter(matmul(lax.slice_in_dim(inverse, 0, rows_here * lax.axis...  64.9 us
  transfers between devices with their start and end apart: 6, of which 5 were waited for; matrix products, arithmetic and copies ran while one was open for 9% of the time, Pallas kernels for 0%

commit v1 on v0

--- a/solution.py
+++ b/solution.py
@@ -9,7 +9,7 @@
 
 def spread(value, axis, source):
     kept = jnp.where(lax.axis_index(axis) == source, value, 0).astype(value.dtype)
-    return lax.psum(kept, axis)
+    return lax.all_gather(kept, axis).sum(axis=0)
 
 
 def matmul(left, right):

time: 950 us -> 1010 us (1.063)
  local copies, waits for them, and re-layouts: 310 us -> 339 us
  other arithmetic: 15.3 us -> 35.2 us
    all_gather x0 -> x2, waiting for transfers between devices: none -> 147 us  [spread(): return lax.all_gather(kept, axis).sum(axis=0)]
    psum x1 -> x0, waiting for transfers between devices: 137 us -> none  [spread(): return lax.psum(kept, axis)]
    all_gather x0 -> x2, local copies, waits for them, and re-layouts: none -> 31.4 us  [spread(): return lax.all_gather(kept, axis).sum(axis=0)]
    reduce_sum x0 -> x2, other arithmetic: none -> 19.8 us  [spread(): return lax.all_gather(kept, axis).sum(axis=0)]
  transfers between devices with their start and end apart: 6 -> 7, of which waited for: 5 -> 6; matrix products, arithmetic and copies ran while one was open for 9% -> 21% of each run, Pallas kernels for 0% -> 0%
where the time goes in v1:
time: 1010 us
  waiting for transfers between devices  469 us (46%)
  local copies, waits for them, and re-layouts  339 us (34%)
  matrix products  152 us (15%)
  other arithmetic  35.2 us (3%)
  between operations  14.4 us (1%)
    gather x2, local copies, waits for them, and re-layouts, local_mask(): flags = jnp.repeat(blocks, BLK, total_repeat_length=blocks.shape[0] * BLK)  304 us
    dot_general x9, matrix products, matmul(): jnp.dot(left, right, precision=HIGHEST, preferred_element_type=jnp.float32)  152 us
    all_gather x2, waiting for transfers between devices, spread(): return lax.all_gather(kept, axis).sum(axis=0)  147 us
    psum x1, waiting for transfers between devices, per_device(): lax.psum((parent_local, cross_local, image_local), ('row', 'col'))  129 us
    all_gather x2, waiting for transfers between devices, apply_inverse(): block_rows = lax.all_gather(panel, 'col', axis=0, tiled=True)  128 us
    reduce_scatter x2, waiting for transfers between devices, apply_inverse(): lax.psum_scatter(matmul(lax.slice_in_dim(inverse, 0, rows_here * lax.axis...  65.2 us
    all_gather x2, local copies, waits for them, and re-layouts, spread(): return lax.all_gather(kept, axis).sum(axis=0)  31.4 us
  transfers between devices with their start and end apart: 7, of which 6 were waited for; matrix products, arithmetic and copies ran while one was open for 21% of the time, Pallas kernels for 0%

profile of v1, /device:TPU:0, one launch (start us, length us, event | category | flops | bytes accessed | tf_op | source)
XLA Modules:
  0.0 1009.9 jit_solution(2501764447730200692)
XLA Ops:
  7.3 0.8 add_bitcast_fusion.1
  8.0 1.9 scatter_custom_fusion
  11.1 151.8 %gather_fusion = s32[24576]{0:T(1024)S(1)} fusion(s32[192]{0:T(256)S(1)} %copy-done.1, s32[24576]{0:T(1024)S(1)} %fusion.5), kind=kCustom, calls=%fused_computation.clone | custom fusion | bytes 294912 | tf_op jit(solution)/shard_map/jit(_take)/gather | solution.py:20
  163.0 151.8 %gather_fusion.1 = s32[24576]{0:T(1024)S(1)} fusion(s32[192]{0:T(256)S(1)} %copy-done.2, s32[24576]{0:T(1024)S(1)} %fusion.5), kind=kCustom, calls=%fused_computation.1.clone | custom fusion | bytes 294912 | tf_op jit(solution)/shard_map/jit(_take)/gather | solution.py:20
  315.1 0.9 broadcast_multiply_fusion.1
  316.4 0.9 broadcast_multiply_fusion
  317.5 66.2 %all-gather.7.cloned.1.call-done = f32[6144,256]{0,1:T(8,128)} async-done(((f32[768,256]{0,1:T(8,128)}), f32[6144,256]{0,1:T(8,128)}) %all-gather.7.cloned.1.call-update) | async-done | bytes 6291472 | tf_op jit(solution)/shard_map/all_gather | solution.py:35
  383.7 3.9 dynamic-slice_select_fusion.1
  387.7 61.5 %all-gather.9.cloned.1.call-done = f32[6144,256]{0,1:T(8,128)} async-done(((f32[768,256]{0,1:T(8,128)}), f32[6144,256]{0,1:T(8,128)}) %all-gather.9.cloned.1.call-update) | async-done | bytes 6291472 | tf_op jit(solution)/shard_map/all_gather | solution.py:35
  449.2 3.8 dynamic-slice_select_fusion
  453.1 119.0 %all-gather.11.cloned.1.call-done = f32[12288,256]{0,1:T(8,128)} async-done(((f32[3072,256]{0,1:T(8,128)}), f32[12288,256]{0,1:T(8,128)}) %all-gather.11.cloned.1.call-update) | async-done | bytes 12582928 | tf_op jit(solution)/shard_map/all_gather | solution.py:12
  572.1 15.9 %reshape.115 = f32[4,3072,256]{1,0,2:T(4,128)} reshape(f32[12288,256]{0,1:T(8,128)} %all-gather.11.cloned.1.call-done) | data formatting | bytes 25165824 | tf_op jit(solution)/shard_map/all_gather | solution.py:12
  588.1 9.9 reduce_sum.18
  597.9 70.2 %convolution_bitcast_fusion.1 = f32[6144,256]{0,1:T(8,128)} fusion(f32[3072,256]{0,1:T(8,128)S(1)} %reduce_sum.18, f32[6144,3072]{1,0:T(8,128)} %param.14), kind=kOutput, calls=%fused_computation.4 | convolution fusion | flops 57982058496 | bytes 84934656 | tf_op jit(solution)/shard_map/dot_general | solution.py:16
  668.2 28.1 %all-gather.13.cloned.1.call-done = f32[12288,256]{0,1:T(8,128)} async-done(((f32[3072,256]{0,1:T(8,128)}), f32[12288,256]{0,1:T(8,128)}) %all-gather.13.cloned.1.call-update) | async-done | bytes 12582928 | tf_op jit(solution)/shard_map/all_gather | solution.py:12
  696.3 15.5 %reshape.116 = f32[4,3072,256]{1,0,2:T(4,128)} reshape(f32[12288,256]{0,1:T(8,128)} %all-gather.13.cloned.1.call-done) | data formatting | bytes 25165824 | tf_op jit(solution)/shard_map/all_gather | solution.py:12
  711.8 10.0 reduce_sum.19
  721.8 70.1 %convolution_bitcast_fusion = f32[6144,256]{0,1:T(8,128)} fusion(f32[3072,256]{0,1:T(8,128)S(1)} %reduce_sum.19, f32[6144,3072]{1,0:T(8,128)} %param.14), kind=kOutput, calls=%fused_computation.3 | convolution fusion | flops 57982058496 | bytes 84934656 | tf_op jit(solution)/shard_map/dot_general | solution.py:16
  792.2 1.4 multiply_negate_fusion
  793.6 1.5 fusion.11
  795.1 1.5 fusion.10
  796.7 65.1 %reduce-scatter.5.cloned.1.call-done = f32[768,256]{0,1:T(8,128)} async-done(((f32[6144,256]{0,1:T(8,128)}), f32[768,256]{0,1:T(8,128)}) %reduce-scatter.5.cloned.1.call-update) | async-done | bytes 786448 | tf_op jit(solution)/shard_map/reduce_scatter | solution.py:38
  861.8 2.7 fusion.12
  864.6 1.1 copy.41
  865.8 2.0 fusion.1
  867.8 1.1 copy.42
  868.9 128.6 %all-reduce.5.cloned.1.call-done = (f32[256,256]{1,0:T(8,128)}, f32[256,256]{1,0:T(8,128)}, f32[256,256]{0,1:T(8,128)}) async-done(((f32[256,256]{1,0:T(8,128)}, f32[256,256]{1,0:T(8,128)}, f32[256,256]{0,1:T(8,128)}), (f32[256,256]{1,0:T(8,128)}, f32[256,256]{1,0:T(8,128)}, f32[256,256]{0,1:T(8,128)})) %all-reduce.5.cloned.1.call-update) | async-done | bytes 786448 | tf_op jit(solution)/shard_map/psum | solution.py:69
  997.5 1.0 sub.20
  998.5 1.4 fusion.4
  999.9 0.6 fusion.3
  1000.6 1.6 fusion.2
  1002.2 0.8 copy.43
  (58 shorter events, 2.7 us)
Async XLA Ops:
  7.2 858.6 %copy-start = (f32[256,256]{1,0:T(8,128)S(1)}, f32[256,256]{1,0:T(8,128)}, u32[]{:S(2)}) copy-start(f32[256,256]{1,0:T(8,128)} %param.17) | copy-start | bytes 786436
  7.2 3.9 copy-start.1
  7.2 376.5 %all-gather.7.cloned.1.call-start = ((), (), s32[]{:S(2)}) async-start(), calls=%async_computation.2 | async-start | bytes 7077888 | tf_op jit(solution)/shard_map/all_gather | solution.py:35
  11.1 151.8 %copy-start.2 = (s32[192]{0:T(256)S(1)}, s32[192]{0:T(256)}, u32[]{:S(2)}) copy-start(s32[192]{0:T(256)} %param.21) | copy-start | bytes 2308
  162.9 151.8 %copy-start.7 = (f32[768,256]{1,0:T(8,128)S(1)}, f32[768,256]{1,0:T(8,128)}, u32[]{:S(2)}) copy-start(f32[768,256]{1,0:T(8,128)} %param.15) | copy-start | bytes 2359300
  162.9 153.2 %copy-start.8 = (f32[768,256]{1,0:T(8,128)S(1)}, f32[768,256]{1,0:T(8,128)}, u32[]{:S(2)}) copy-start(f32[768,256]{1,0:T(8,128)} %param.16) | copy-start | bytes 2359300
  316.1 133.1 %all-gather.9.cloned.1.call-start = ((), (), s32[]{:S(2)}) async-start(), calls=%async_computation.4 | async-start | bytes 7077888 | tf_op jit(solution)/shard_map/all_gather | solution.py:35
  317.4 254.7 %all-gather.11.cloned.1.call-start = ((), (), s32[]{:S(2)}) async-start(), calls=%async_computation.6 | async-start | bytes 15728640 | tf_op jit(solution)/shard_map/all_gather | solution.py:12
  387.6 308.6 %all-gather.13.cloned.1.call-start = ((), (), s32[]{:S(2)}) async-start(), calls=%async_computation.7 | async-start | bytes 15728640 | tf_op jit(solution)/shard_map/all_gather | solution.py:12
  453.1 339.1 %reduce-scatter.3.cloned.1.call-start = ((), (), s32[]{:S(2)}) async-start(), calls=%async_computation.3 | async-start | bytes 7077888 | tf_op jit(solution)/shard_map/reduce_scatter | solution.py:38
  668.1 193.7 %reduce-scatter.5.cloned.1.call-start = ((), (), s32[]{:S(2)}) async-start(), calls=%async_computation.5 | async-start | bytes 7077888 | tf_op jit(solution)/shard_map/reduce_scatter | solution.py:38
  791.8 1.7 copy-start.3
  791.8 3.3 copy-start.4
  791.8 72.6 %copy-start.10 = (f32[256,256]{1,0:T(8,128)S(1)}, f32[256,256]{1,0:T(8,128)}, u32[]{:S(2)}) copy-start(f32[256,256]{1,0:T(8,128)} %param.19) | copy-start | bytes 786436
  791.9 205.6 %all-reduce.5.cloned.1.call-start = ((), (), s32[]{:S(2)}) async-start(), calls=%async_computation.8 | async-start | bytes 1572864 | tf_op jit(solution)/shard_map/psum | solution.py:69
  793.6 203.9 %copy-start.9 = (f32[256,256]{1,0:T(8,128)S(1)}, f32[256,256]{1,0:T(8,128)}, u32[]{:S(2)}) copy-start(f32[256,256]{1,0:T(8,128)} %param.18) | copy-start | bytes 786436
  998.5 4.5 copy-start.5
  999.9 3.1 copy-start.6
Sparse Core Ops, SparseCore 0:
  316.2 67.4 all-gather.6
  385.9 63.3 all-gather.8
  451.1 121.0 all-gather.10
  573.8 122.3 all-gather.12
  698.4 69.7 reduce-scatter.2
  792.0 69.7 reduce-scatter.4
  867.9 129.5 all-reduce.4
